TPU v7x, 1024 devices: a whole 4x4x32 slice. The times are simulated.
1024 devices in a mesh: energy: 64 (over z_lo, y), mom: 16 (over z_hi, x, core).
Axes of the slice: x: 4, y: 4, z: 32 (z_hi: 2, z_lo: 16; z = z_hi * 16 + z_lo), core: 2. Of those that a mesh axis runs over, the one named last changes fastest.
Arguments:
- green_blocks: bfloat16 [2, 64, 16, 64, 64, 128], P(None, 'energy', 'mom'), may hold values from -6 to 6
- bond_grad: bfloat16 [64, 4, 64, 64], replicated, may hold values from -0.5 to 0.5
- neighbours: int32 [64, 4], replicated, may hold values from 0 to 63
- occupation: float32 [4], replicated, may hold values from 0.05 to 1
- energy_shift: int32 [4], replicated, may hold values from 1 to 16, as said below
- mom_weight: float32 [16, 3], P('mom'), may hold values from 0.3 to 1
Outputs:
- broadening: bfloat16 [64, 16, 64, 64, 128], P(None, 'mom', 'energy')
Inputs may be any that keep to these rules, and one draw needn't show every extreme that they name: `energy_shift`: energy offsets of at least one point; the largest equals 16. `neighbours`: atom indices; repeats possible.
All inputs are finite; a program needn't handle non-finite values.
Results may differ from a plain program's by a relative error of at most 0.0064.
Values may be sent and summed in bfloat16 or wider, within the bound.
No kernel may reach another device: no remote copies, remote signals or barrier semaphores. Data moves between devices by JAX's collectives and lax.ppermute only.
A program may use at most 64 MiB of HBM per device.

v0:
```python
import jax
import jax.numpy as jnp
from jax import lax
from jax.sharding import PartitionSpec as P


def passed_along(value, axis, steps):
    count = lax.axis_size(axis)
    pairs = [(source, (source + steps) % count) for source in range(count)]
    return lax.ppermute(value, axis, pairs)


def sandwich(blocks, bond_grad, neighbours):
    orbitals = bond_grad.shape[-1]
    slots = neighbours.shape[1]

    def one_kind(kind_blocks):

        def add_slot(slot, summed):
            indices = lax.dynamic_index_in_dim(neighbours, slot, 1, keepdims=False)
            gradient = lax.dynamic_index_in_dim(bond_grad, slot, 1, keepdims=False)
            picked = jnp.take(kind_blocks, indices, axis=-3)
            left_product = jnp.einsum(
                "ami,...aic->...amc", gradient, picked, preferred_element_type=jnp.float32
            ).astype(jnp.bfloat16)
            halves = left_product.reshape(left_product.shape[:-1] + (2, orbitals))
            sandwiched = jnp.einsum(
                "...amhi,aji->...amhj", halves, gradient, preferred_element_type=jnp.float32
            )
            return summed + sandwiched.reshape(left_product.shape)

        summed = lax.fori_loop(0, slots, add_slot, jnp.zeros(kind_blocks.shape, jnp.float32))
        return summed.astype(jnp.bfloat16)

    return lax.map(one_kind, blocks)


def combine(from_below, local_part, from_above, mom_weight):
    weights = [mom_weight[:, column].reshape(1, 1, -1, 1, 1, 1) for column in range(3)]
    mixed = weights[0] * from_below.astype(jnp.float32) + weights[1] * local_part.astype(
        jnp.float32
    )
    mixed = mixed + weights[2] * from_above.astype(jnp.float32)
    return mixed.astype(jnp.bfloat16)


def transpose_layout(blocks):
    return lax.all_to_all(blocks, "energy", split_axis=3, concat_axis=1, tiled=True)


def mix_kind(slab, occupation, energy_shift, lower_factor, upper_factor):
    energies = slab.shape[0]
    furthest = energies // 4
    widths = [(0, 0)] * slab.ndim
    widths[0] = (furthest, furthest)
    padded = jnp.pad(slab, widths)
    total = jnp.zeros(slab.shape, jnp.float32)
    for phonon in range(occupation.shape[0]):
        offset = energy_shift[phonon]
        filled = occupation[phonon]
        shifted_down = lax.dynamic_slice_in_dim(padded, furthest - offset, energies, axis=0).astype(
            jnp.float32
        )
        shifted_up = lax.dynamic_slice_in_dim(padded, furthest + offset, energies, axis=0).astype(
            jnp.float32
        )
        total = (
            total + (filled + lower_factor) * shifted_down + (filled + upper_factor) * shifted_up
        )
    return total


def energy_mix(mixed, occupation, energy_shift):
    greater = mix_kind(mixed[1], occupation, energy_shift, 1.0, 0.0)
    lesser = mix_kind(mixed[0], occupation, energy_shift, 0.0, 1.0)
    return (greater - lesser).astype(jnp.bfloat16)


def on_device(green_blocks, bond_grad, neighbours, occupation, energy_shift, mom_weight):
    local_part = sandwich(green_blocks, bond_grad, neighbours)
    moved = transpose_layout(local_part)
    from_below = passed_along(moved, "mom", 1)
    from_above = passed_along(moved, "mom", -1)
    mixed = combine(from_below, moved, from_above, mom_weight)
    return energy_mix(mixed, occupation, energy_shift)


def solution(mesh):
    in_specs = (P(None, "energy", "mom", None, None, None), P(), P(), P(), P(), P("mom", None))
    out_specs = P(None, "mom", "energy", None, None)
    return jax.shard_map(
        on_device, mesh=mesh, in_specs=in_specs, out_specs=out_specs, check_vma=False
    )
```

profile of v0, /device:TPU:16, one launch (start us, length us, event | category | flops | bytes accessed | tf_op | source)
XLA Modules:
  0.0 592.0 jit_solution(2285265272549453516)
XLA Ops:
  0.0 5.4 copy.12
  5.4 138.4 %while.25 = (s32[]{:T(128)}, bf16[2,1,1,64,64,128]{5,4,0,2,1,3:T(8,128)(2,1)}, bf16[2,1,1,64,64,128]{5,4,3,2,1,0:T(8,128)(2,1)}, bf16[64,4,64,64]{3,2,0,1:T(8,12...) while((s32[]{:T(128)}, bf16[2,1,1,64,64,128]{5,4,0,2,1,3:T(8,128)(2,1)}, ...), condition=%wide.region_3.4_spmd, body=%wide.region_0.3_spmd.sunk | while | flops 136840576 | bytes 35657168 | solution.py:35
  5.4 1.3 dynamic-slice_bitcast_fusion.2
  6.7 63.1 %while.26 = (s32[]{:T(128)}, f32[1,1,64,64,128]{3,4,2,1,0:T(8,128)}, bf16[64,4,64,64]{3,2,0,1:T(8,128)(2,1)}, s32[64,4]{0,1:T(4,128)}, bf16[1,1,64,64,128]{4,3,2,1,0:T(8,128)(2,1)S(1)}, /*index=5*/s32[]{:T(128)}, s32[]{:T(128)}) while((s32[]{:T(128)}, f32[1,1,64,64,128]{3,4,2,1,0:T(8,128)}, bf16[64,4,64,64]{3,2,0,1:T(8,128)(2,1)}, ...), condition=%wide.region_2.2_spmd.clone, body=%wide.region_1.1_spmd.clone.sunk | while | flops 136316288 | bytes 26219812 | solution.py:32
  6.8 0.7 and_bitcast_fusion.2
  7.5 0.7 gather_fusion
  8.2 1.7 fusion.27
  10.0 0.8 reshape.122
  10.8 5.3 fusion.28
  16.1 5.5 select_add_fusion.2
  21.6 0.7 and_bitcast_fusion.2
  22.3 0.7 gather_fusion
  23.1 1.7 fusion.27
  24.8 0.8 reshape.122
  25.7 5.3 fusion.28
  31.0 6.7 %select_add_fusion.2 = f32[1,1,64,64,128]{3,4,2,1,0:T(8,128)} fusion(f32[1,1,64,64,128]{3,4,2,1,0:T(8,128)} %bitcast.78, f32[1,1,64,64,128]{3,4,2,1,0:T(8,128)} %get-tuple-element.277, pred[]{:T(512)S(6)} %compare.5), kind=kLoop, calls=%fused_computation.1.clone.1 | loop fusion | flops 1048576 | bytes 6291457 | tf_op jit(solution)/shard_map/while/body/eval_jaxpr/while/body/eval_jaxpr/add | solution.py:30
  37.7 0.7 and_bitcast_fusion.2
  38.4 0.7 gather_fusion
  39.2 1.7 fusion.27
  40.9 0.8 reshape.122
  41.7 5.3 fusion.28
  47.1 6.7 %select_add_fusion.2 = f32[1,1,64,64,128]{3,4,2,1,0:T(8,128)} fusion(f32[1,1,64,64,128]{3,4,2,1,0:T(8,128)} %bitcast.78, f32[1,1,64,64,128]{3,4,2,1,0:T(8,128)} %get-tuple-element.277, pred[]{:T(512)S(6)} %compare.5), kind=kLoop, calls=%fused_computation.1.clone.1 | loop fusion | flops 1048576 | bytes 6291457 | tf_op jit(solution)/shard_map/while/body/eval_jaxpr/while/body/eval_jaxpr/add | solution.py:30
  53.8 0.7 and_bitcast_fusion.2
  54.5 0.7 gather_fusion
  55.3 1.7 fusion.27
  57.0 0.8 reshape.122
  57.8 5.3 fusion.28
  63.1 6.7 %select_add_fusion.2 = f32[1,1,64,64,128]{3,4,2,1,0:T(8,128)} fusion(f32[1,1,64,64,128]{3,4,2,1,0:T(8,128)} %bitcast.78, f32[1,1,64,64,128]{3,4,2,1,0:T(8,128)} %get-tuple-element.277, pred[]{:T(512)S(6)} %compare.5), kind=kLoop, calls=%fused_computation.1.clone.1 | loop fusion | flops 1048576 | bytes 6291457 | tf_op jit(solution)/shard_map/while/body/eval_jaxpr/while/body/eval_jaxpr/add | solution.py:30
  69.9 2.6 convert_bitcast_fusion.2
  72.4 0.9 copy.26
  73.4 1.3 constant_dynamic-update-slice_fusion.2
  74.6 1.3 dynamic-slice_bitcast_fusion.2
  75.9 63.1 %while.26 = (s32[]{:T(128)}, f32[1,1,64,64,128]{3,4,2,1,0:T(8,128)}, bf16[64,4,64,64]{3,2,0,1:T(8,128)(2,1)}, s32[64,4]{0,1:T(4,128)}, bf16[1,1,64,64,128]{4,3,2,1,0:T(8,128)(2,1)S(1)}, /*index=5*/s32[]{:T(128)}, s32[]{:T(128)}) while((s32[]{:T(128)}, f32[1,1,64,64,128]{3,4,2,1,0:T(8,128)}, bf16[64,4,64,64]{3,2,0,1:T(8,128)(2,1)}, ...), condition=%wide.region_2.2_spmd.clone, body=%wide.region_1.1_spmd.clone.sunk | while | flops 136316288 | bytes 26219812 | solution.py:32
  76.0 0.7 and_bitcast_fusion.2
  76.7 0.7 gather_fusion
  77.5 1.7 fusion.27
  79.2 0.8 reshape.122
  80.0 5.3 fusion.28
  85.3 5.5 select_add_fusion.2
  91.5 0.7 gather_fusion
  92.3 1.7 fusion.27
  94.0 0.8 reshape.122
  94.9 5.3 fusion.28
  100.2 6.7 %select_add_fusion.2 = f32[1,1,64,64,128]{3,4,2,1,0:T(8,128)} fusion(f32[1,1,64,64,128]{3,4,2,1,0:T(8,128)} %bitcast.78, f32[1,1,64,64,128]{3,4,2,1,0:T(8,128)} %get-tuple-element.277, pred[]{:T(512)S(6)} %compare.5), kind=kLoop, calls=%fused_computation.1.clone.1 | loop fusion | flops 1048576 | bytes 6291457 | tf_op jit(solution)/shard_map/while/body/eval_jaxpr/while/body/eval_jaxpr/add | solution.py:30
  107.6 0.7 gather_fusion
  108.4 1.7 fusion.27
  110.1 0.8 reshape.122
  111.0 5.3 fusion.28
  116.3 6.7 %select_add_fusion.2 = f32[1,1,64,64,128]{3,4,2,1,0:T(8,128)} fusion(f32[1,1,64,64,128]{3,4,2,1,0:T(8,128)} %bitcast.78, f32[1,1,64,64,128]{3,4,2,1,0:T(8,128)} %get-tuple-element.277, pred[]{:T(512)S(6)} %compare.5), kind=kLoop, calls=%fused_computation.1.clone.1 | loop fusion | flops 1048576 | bytes 6291457 | tf_op jit(solution)/shard_map/while/body/eval_jaxpr/while/body/eval_jaxpr/add | solution.py:30
  123.7 0.7 gather_fusion
  124.5 1.7 fusion.27
  126.2 0.8 reshape.122
  127.0 5.3 fusion.28
  132.4 6.7 %select_add_fusion.2 = f32[1,1,64,64,128]{3,4,2,1,0:T(8,128)} fusion(f32[1,1,64,64,128]{3,4,2,1,0:T(8,128)} %bitcast.78, f32[1,1,64,64,128]{3,4,2,1,0:T(8,128)} %get-tuple-element.277, pred[]{:T(512)S(6)} %compare.5), kind=kLoop, calls=%fused_computation.1.clone.1 | loop fusion | flops 1048576 | bytes 6291457 | tf_op jit(solution)/shard_map/while/body/eval_jaxpr/while/body/eval_jaxpr/add | solution.py:30
  139.1 2.6 convert_bitcast_fusion.2
  141.6 0.9 copy.26
  142.6 1.2 constant_dynamic-update-slice_fusion.2
  143.8 219.4 %all_to_all.12 = bf16[2,1,1,64,64,128]{5,4,0,2,1,3:T(8,128)(2,1)S(1)} all-to-all(bf16[2,1,1,64,64,128]{5,4,0,2,1,3:T(8,128)(2,1)} %get-tuple-element.126), channel_id=1, replica_groups=mesh['energy'=64,'mom'=16] {'energy'}, dimensions={3} | all-to-all | bytes 4194304 | tf_op jit(solution)/shard_map/all_to_all | solution.py:48
  363.2 12.4 %collective-permute-start.1 = (bf16[2,64,1,1,64,128]{5,4,0,1,3,2:T(8,128)(2,1)S(1)}, bf16[2,64,1,1,64,128]{5,4,0,1,3,2:T(8,128)(2,1)}, u32[]{:S(2)}, u32[]{:S(2)}) collective-permute-start(bf16[2,64,1,1,64,128]{5,4,0,1,3,2:T(8,128)(2,1)S(1)} %bitcast.80), channel_id=1, source_target_pairs={{0,15},{1,0},{2,1},{3,2},{4,3},{5,4},{6,5},{7,6},{8,7},{9,8},{10,9... | collective-permute-start | bytes 6291464 | tf_op jit(solution)/shard_map/ppermute | solution.py:10
  375.7 1.9 collective-permute-start
  391.9 159.8 %collective-permute-done.1 = bf16[2,64,1,1,64,128]{5,4,0,1,3,2:T(8,128)(2,1)} collective-permute-done((bf16[2,64,1,1,64,128]{5,4,0,1,3,2:T(8,128)(2,1)S(1)}, bf16[2,64,1,1,64,128]{5,4,0,1,3,2:T(8,128)(2,1)}, u32[]{:S(2)}, u32[]{:S(2)}) %collective-permute-start.1) | collective-permute-done | bytes 2097184 | tf_op jit(solution)/shard_map/ppermute | solution.py:10
  551.7 24.4 %collective-permute-done = bf16[2,64,1,1,64,128]{5,4,0,1,3,2:T(8,128)(2,1)} collective-permute-done((bf16[2,64,1,1,64,128]{5,4,0,1,3,2:T(8,128)(2,1)S(1)}, bf16[2,64,1,1,64,128]{5,4,0,1,3,2:T(8,128)(2,1)}, u32[]{:S(2)}, u32[]{:S(2)}) %collective-permute-start) | collective-permute-done | bytes 2097184 | tf_op jit(solution)/shard_map/ppermute | solution.py:10
  576.2 5.6 add_convert_fusion
  582.0 10.0 %fusion.13 = bf16[64,1,1,64,128]{4,3,2,1,0:T(8,128)(2,1)} fusion(s32[]{:T(128)S(6)} %select_n.71, bf16[64,1,1,64,128]{4,3,0,2,1:T(8,128)(2,1)S(1)} %get-tuple-element.178, s32[]{:T(128)S(6)} %select_n.70, s32[]{:T(128)S(6)} %select_n.69, s32[]{:T(128)S(6)} %select_n.68, s32[]{:T(128)S(6)} %select_n.67, s32[]{:T(128)S(6)} %select_n.66, s32[]{:T(128)S(6)} %select_n.65, ...), kind=kLoop, calls=%fused_computation.42 | loop fusion | flops 25165824 | bytes 3145792 | tf_op jit(solution)/shard_map/convert_element_type | solution.py:76
  (56 shorter events, 4.3 us)
Async XLA Ops:
  6.7 1.5 copy-start
  16.1 5.5 copy-start.1
  21.6 1.5 copy-start
  31.0 6.7 %copy-start.1 = (bf16[1,1,64,64,128]{4,3,2,1,0:T(8,128)(2,1)S(1)}, bf16[1,1,64,64,128]{4,3,2,1,0:T(8,128)(2,1)}, u32[]{:S(2)}) copy-start(bf16[1,1,64,64,128]{4,3,2,1,0:T(8,128)(2,1)} %copy-done) | copy-start | bytes 3145732 | tf_op jit(solution)/shard_map/while/body/eval_jaxpr/while
  37.7 1.5 copy-start
  47.1 6.7 %copy-start.1 = (bf16[1,1,64,64,128]{4,3,2,1,0:T(8,128)(2,1)S(1)}, bf16[1,1,64,64,128]{4,3,2,1,0:T(8,128)(2,1)}, u32[]{:S(2)}) copy-start(bf16[1,1,64,64,128]{4,3,2,1,0:T(8,128)(2,1)} %copy-done) | copy-start | bytes 3145732 | tf_op jit(solution)/shard_map/while/body/eval_jaxpr/while
  53.8 1.5 copy-start
  63.1 6.7 %copy-start.1 = (bf16[1,1,64,64,128]{4,3,2,1,0:T(8,128)(2,1)S(1)}, bf16[1,1,64,64,128]{4,3,2,1,0:T(8,128)(2,1)}, u32[]{:S(2)}) copy-start(bf16[1,1,64,64,128]{4,3,2,1,0:T(8,128)(2,1)} %copy-done) | copy-start | bytes 3145732 | tf_op jit(solution)/shard_map/while/body/eval_jaxpr/while
  75.9 1.5 copy-start
  85.3 5.5 copy-start.1
  90.8 1.5 copy-start
  100.2 6.7 %copy-start.1 = (bf16[1,1,64,64,128]{4,3,2,1,0:T(8,128)(2,1)S(1)}, bf16[1,1,64,64,128]{4,3,2,1,0:T(8,128)(2,1)}, u32[]{:S(2)}) copy-start(bf16[1,1,64,64,128]{4,3,2,1,0:T(8,128)(2,1)} %copy-done) | copy-start | bytes 3145732 | tf_op jit(solution)/shard_map/while/body/eval_jaxpr/while
  106.9 1.5 copy-start
  116.3 6.7 %copy-start.1 = (bf16[1,1,64,64,128]{4,3,2,1,0:T(8,128)(2,1)S(1)}, bf16[1,1,64,64,128]{4,3,2,1,0:T(8,128)(2,1)}, u32[]{:S(2)}) copy-start(bf16[1,1,64,64,128]{4,3,2,1,0:T(8,128)(2,1)} %copy-done) | copy-start | bytes 3145732 | tf_op jit(solution)/shard_map/while/body/eval_jaxpr/while
  123.0 1.5 copy-start
  132.3 6.7 %copy-start.1 = (bf16[1,1,64,64,128]{4,3,2,1,0:T(8,128)(2,1)S(1)}, bf16[1,1,64,64,128]{4,3,2,1,0:T(8,128)(2,1)}, u32[]{:S(2)}) copy-start(bf16[1,1,64,64,128]{4,3,2,1,0:T(8,128)(2,1)} %copy-done) | copy-start | bytes 3145732 | tf_op jit(solution)/shard_map/while/body/eval_jaxpr/while
  143.8 233.8 %copy-start.2 = (s32[4]{0:T(128)S(1)}, s32[4]{0:T(128)}, u32[]{:S(2)}) copy-start(s32[4]{0:T(128)} %param.14) | copy-start | bytes 52
  143.8 244.3 %copy-start.3 = (f32[4]{0:T(128)S(1)}, f32[4]{0:T(128)}, u32[]{:S(2)}) copy-start(f32[4]{0:T(128)} %param.13) | copy-start | bytes 52
  143.8 247.5 %copy-start.4 = (f32[1,3]{1,0:T(1,128)S(1)}, f32[1,3]{1,0:T(1,128)}, u32[]{:S(2)}) copy-start(f32[1,3]{1,0:T(1,128)} %param.15) | copy-start | bytes 40
  363.2 188.5 %collective-permute-start.1 = (bf16[2,64,1,1,64,128]{5,4,0,1,3,2:T(8,128)(2,1)S(1)}, bf16[2,64,1,1,64,128]{5,4,0,1,3,2:T(8,128)(2,1)}, u32[]{:S(2)}, u32[]{:S(2)}) collective-permute-start(bf16[2,64,1,1,64,128]{5,4,0,1,3,2:T(8,128)(2,1)S(1)} %bitcast.80), channel_id=1, source_target_pairs={{0,15},{1,0},{2,1},{3,2},{4,3},{5,4},{6,5},{7,6},{8,7},{9,8},{10,9... | collective-permute-start | bytes 6291464 | tf_op jit(solution)/shard_map/ppermute | solution.py:10
  375.7 200.5 %collective-permute-start = (bf16[2,64,1,1,64,128]{5,4,0,1,3,2:T(8,128)(2,1)S(1)}, bf16[2,64,1,1,64,128]{5,4,0,1,3,2:T(8,128)(2,1)}, u32[]{:S(2)}, u32[]{:S(2)}) collective-permute-start(bf16[2,64,1,1,64,128]{5,4,0,1,3,2:T(8,128)(2,1)S(1)} %bitcast.81), channel_id=1, source_target_pairs={{0,1},{1,2},{2,3},{3,4},{4,5},{5,6},{6,7},{7,8},{8,9},{9,10},{10,1... | collective-permute-start | bytes 6291464 | tf_op jit(solution)/shard_map/ppermute | solution.py:10
where the time goes:
time: 594 us; the launch traced here: 592 us
  blocking collectives  219 us (37%)
  waiting for transfers between devices  184 us (31%)
  other arithmetic  77.6 us (13%)
  matrix products  56.3 us (9%)
  local copies, waits for them, and re-layouts  27.3 us (5%)
  starting transfers between devices  14.3 us (2%)
  between operations  12.4 us (2%)
    all_to_all x1, blocking collectives, transpose_layout(): lax.all_to_all(blocks, 'energy', split_axis=3, concat_axis=1, tiled=True)  219 us
    ppermute x2, waiting for transfers between devices, passed_along(): return lax.ppermute(value, axis, pairs)  184 us
    add x8, other arithmetic, add_slot(): return summed + sandwiched.reshape(left_product.shape)  51.3 us
    dot_general x8, matrix products, add_slot(): jnp.einsum('...amhi,aji->...amhj', halves, gradient, preferred_element_ty...  42.5 us
    ppermute x2, starting transfers between devices, passed_along(): return lax.ppermute(value, axis, pairs)  14.3 us
    dot_general x8, matrix products, add_slot(): jnp.einsum('ami,...aic->...amc', gradient, picked, preferred_element_type...  13.8 us
  transfers between devices with their start and end apart: 2, of which 2 were waited for; matrix products, arithmetic and copies ran while one was open for 0% of the time, Pallas kernels for 0%

commit v1 on v0

v1 whole, which is shorter than its diff:
```python
import functools

import jax
import jax.numpy as jnp
from jax import lax
from jax.experimental import pallas as pl
from jax.experimental.pallas import tpu as pltpu
from jax.sharding import PartitionSpec as P

CHUNKS = 1
ATOMS_PER_STEP = 8
FURTHEST = 16


def sandwich_kernel(slots, neighbours_ref, green_ref, bond_ref, *rest):
    out_refs, stacked = rest[:-1], rest[-1]
    per_step, orbitals = bond_ref.shape[0], bond_ref.shape[-1]
    group = pl.program_id(0)
    rows = orbitals // len(out_refs)
    for local in range(per_step):
        atom = group * per_step + local
        lefts = []
        for slot in range(slots):
            source = neighbours_ref[atom * slots + slot]
            blocks = jnp.concatenate([green_ref[0, source], green_ref[1, source]], axis=1)
            lefts.append(
                jnp.dot(
                    bond_ref[local, slot], blocks, preferred_element_type=jnp.float32
                ).astype(jnp.bfloat16)
            )
        buffer = stacked.at[local % 2]
        for part in range(4):
            columns = slice(part * orbitals, (part + 1) * orbitals)
            for pair in range(slots // 2):
                buffer[columns, 2 * pair * orbitals : 2 * (pair + 1) * orbitals] = jnp.concatenate(
                    [lefts[2 * pair][:, columns], lefts[2 * pair + 1][:, columns]], axis=1
                )
        gradient = jnp.concatenate([bond_ref[local, slot] for slot in range(slots)], axis=1)
        total = lax.dot_general(
            buffer[...],
            gradient,
            (((1,), (1,)), ((), ())),
            preferred_element_type=jnp.float32,
        ).astype(jnp.bfloat16)
        for kind in range(2):
            start = 2 * kind * orbitals
            both = jnp.concatenate(
                [total[start : start + orbitals], total[start + orbitals : start + 2 * orbitals]],
                axis=1,
            )
            for chunk, out_ref in enumerate(out_refs):
                out_ref[local, kind] = both[chunk * rows : (chunk + 1) * rows]


def sandwich(green, bond_grad, neighbours, chunks):
    kinds, atoms, orbitals, width = green.shape
    slots = bond_grad.shape[1]
    rows = orbitals // chunks
    per_step = ATOMS_PER_STEP
    block = pl.BlockSpec((per_step, kinds, rows, width), lambda i, n: (i, 0, 0, 0))
    return pl.pallas_call(
        functools.partial(sandwich_kernel, slots),
        grid_spec=pltpu.PrefetchScalarGridSpec(
            num_scalar_prefetch=1,
            grid=(atoms // per_step,),
            in_specs=[
                pl.BlockSpec((kinds, atoms, orbitals, width), lambda i, n: (0, 0, 0, 0)),
                pl.BlockSpec((per_step, slots, orbitals, orbitals), lambda i, n: (i, 0, 0, 0)),
            ],
            out_specs=[block] * chunks,
            scratch_shapes=[pltpu.VMEM((2, 4 * orbitals, slots * orbitals), jnp.bfloat16)],
        ),
        out_shape=[jax.ShapeDtypeStruct((atoms, kinds, rows, width), jnp.bfloat16)] * chunks,
        compiler_params=pltpu.CompilerParams(vmem_limit_bytes=32 << 20),
        name="sandwich",
    )(neighbours.reshape(-1), green, bond_grad)


def energy_kernel(modes, per_step, shift_ref, occupation_ref, moved_ref, out_ref, padded):
    energies, kinds, rows, width = moved_ref.shape
    step = pl.program_id(0)

    @pl.when(step == 0)
    def _():
        zeros = jnp.zeros((FURTHEST, kinds, rows, width), jnp.bfloat16)
        padded[pl.ds(0, FURTHEST)] = zeros
        padded[pl.ds(FURTHEST + energies, FURTHEST)] = zeros
        padded[pl.ds(FURTHEST, energies)] = moved_ref[...]

    @pl.loop(0, per_step)
    def _(local):
        centre = step * per_step + local + FURTHEST
        total = jnp.zeros((rows, width), jnp.float32)
        for mode in range(modes):
            filled = occupation_ref[mode]
            down = padded[centre - shift_ref[mode]].astype(jnp.float32)
            up = padded[centre + shift_ref[mode]].astype(jnp.float32)
            total = total + (filled + 1.0) * (down[1] - up[0]) + filled * (up[1] - down[0])
        out_ref[local] = total.astype(jnp.bfloat16)


def energy_mix(moved, occupation, energy_shift):
    energies, kinds, rows, width = moved.shape
    per_step = 8
    return pl.pallas_call(
        functools.partial(energy_kernel, occupation.shape[0], per_step),
        grid_spec=pltpu.PrefetchScalarGridSpec(
            num_scalar_prefetch=2,
            grid=(energies // per_step,),
            in_specs=[
                pl.BlockSpec((energies, kinds, rows, width), lambda i, s, o: (0, 0, 0, 0))
            ],
            out_specs=pl.BlockSpec((per_step, rows, width), lambda i, s, o: (i, 0, 0)),
            scratch_shapes=[
                pltpu.VMEM((energies + 2 * FURTHEST, kinds, rows, width), jnp.bfloat16)
            ],
        ),
        out_shape=jax.ShapeDtypeStruct((energies, rows, width), jnp.bfloat16),
        compiler_params=pltpu.CompilerParams(vmem_limit_bytes=32 << 20),
        name="energy_mix",
    )(energy_shift, occupation, moved)


def passed_along(value, axis, steps):
    count = lax.axis_size(axis)
    pairs = [(source, (source + steps) % count) for source in range(count)]
    return lax.ppermute(value, axis, pairs)


def combine(from_below, own, from_above, weights):
    mixed = weights[0, 0] * from_below.astype(jnp.float32) + weights[0, 1] * own.astype(jnp.float32)
    return (mixed + weights[0, 2] * from_above.astype(jnp.float32)).astype(jnp.bfloat16)


def on_device(green_blocks, bond_grad, neighbours, occupation, energy_shift, mom_weight):
    green = green_blocks[:, 0, 0]
    local_parts = sandwich(green, bond_grad, neighbours, CHUNKS)
    outs = []
    for part in local_parts:
        moved = lax.all_to_all(part, "energy", split_axis=0, concat_axis=0, tiled=True)
        own = energy_mix(moved, occupation, energy_shift)
        below = passed_along(own, "mom", 1)
        above = passed_along(own, "mom", -1)
        outs.append(combine(below, own, above, mom_weight))
    result = outs[0] if CHUNKS == 1 else jnp.concatenate(outs, axis=1)
    return result[:, None, None]


def solution(mesh):
    in_specs = (P(None, "energy", "mom", None, None, None), P(), P(), P(), P(), P("mom", None))
    out_specs = P(None, "mom", "energy", None, None)
    return jax.shard_map(
        on_device, mesh=mesh, in_specs=in_specs, out_specs=out_specs, check_vma=False
    )
```

time: 594 us -> 365 us (0.61)
  the two profiles are of different devices: /device:TPU:16 before, /device:TPU:23 now
where the time goes in v1:
time: 365 us
  blocking collectives  218 us (60%)
  waiting for transfers between devices  108 us (30%)
  starting transfers between devices  15.1 us (4%)
  Pallas kernels  14.8 us (4%)
  local copies, waits for them, and re-layouts  5.32 us (1%)
    all_to_all x1, blocking collectives, on_device(): lax.all_to_all(part, 'energy', split_axis=0, concat_axis=0, tiled=True)  218 us
    ppermute x2, waiting for transfers between devices, passed_along(): return lax.ppermute(value, axis, pairs)  108 us
    ppermute x2, starting transfers between devices, passed_along(): return lax.ppermute(value, axis, pairs)  15.1 us
    pallas_call x1, Pallas kernels, sandwich(): pl.pallas_call(functools.partial(sandwich_kernel, slots), grid_spec=pltpu...  10.4 us
  transfers between devices with their start and end apart: 2, of which 2 were waited for; matrix products, arithmetic and copies ran while one was open for 0% of the time, Pallas kernels for 0%

profile of v1, /device:TPU:23, one launch (start us, length us, event | category | flops | bytes accessed | tf_op | source)
XLA Modules:
  0.0 364.6 jit_solution(3349128151481619385)
XLA Ops:
  0.0 0.8 copy.8
  0.8 0.1 reshape.3.neighbours_ref
  0.9 0.0 copy-start
  0.9 2.2 copy-done
  3.1 0.0 copy-start.1
  3.1 1.6 copy-done.1
  4.7 10.4 %sandwich.1 = bf16[64,2,64,128]{3,2,1,0:T(8,128)(2,1)S(1)} custom-call(s32[256]{0:T(256)S(1)} %reshape.3.neighbours_ref, bf16[2,64,64,128]{3,2,1,0:T(8,128)(2,1)S(1)} %bitcast.8, bf16[64,4,64,64]{3,2,1,0:T(8,128)(2,1)S(1)} %copy-done), custom_call_target="tpu_custom_call" | custom-call | tf_op jit(solution)/shard_map/sandwich/pallas_call | solution.py:61
  15.1 0.0 copy-start.2
  15.1 0.0 copy-start.3
  15.1 218.2 %all_to_all.5.moved_ref = bf16[64,2,64,128]{3,2,1,0:T(8,128)(2,1)S(1)} all-to-all(bf16[64,2,64,128]{3,2,1,0:T(8,128)(2,1)S(1)} %sandwich.1), channel_id=1, replica_groups=mesh['energy'=64,'mom'=16] {'energy'}, dimensions={0} | all-to-all | bytes 4194304 | tf_op jit(solution)/shard_map/all_to_all | solution.py:140
  233.3 0.0 copy-done.2
  233.3 0.0 copy-done.3
  233.3 0.0 copy-start.4
  233.3 4.3 %energy_mix.1 = bf16[64,64,128]{2,1,0:T(8,128)(2,1)S(1)} custom-call(s32[4]{0:T(128)S(1)} %copy-done.2, f32[4]{0:T(128)S(1)} %copy-done.3, bf16[64,2,64,128]{3,2,1,0:T(8,128)(2,1)S(1)} %all_to_all.5.moved_ref), custom_call_target="tpu_custom_call" | custom-call | tf_op jit(solution)/shard_map/energy_mix/pallas_call | solution.py:105
  237.6 13.1 %collective-permute-start = (bf16[64,64,128]{2,1,0:T(8,128)(2,1)S(1)}, bf16[64,64,128]{2,1,0:T(8,128)(2,1)S(1)}, u32[]{:S(2)}, u32[]{:S(2)}) collective-permute-start(bf16[64,64,128]{2,1,0:T(8,128)(2,1)S(1)} %energy_mix.1), channel_id=1, source_target_pairs={{0,1},{1,2},{2,3},{3,4},{4,5},{5,6},{6,7},{7,8},{8,9},{9,10},{10,1... | collective-permute-start | bytes 3145736 | tf_op jit(solution)/shard_map/ppermute | solution.py:127
  250.8 1.9 collective-permute-start.1
  252.7 0.0 copy-done.4
  252.7 0.7 fusion.1
  253.4 82.8 %collective-permute-done = bf16[64,64,128]{2,1,0:T(8,128)(2,1)S(1)} collective-permute-done((bf16[64,64,128]{2,1,0:T(8,128)(2,1)S(1)}, bf16[64,64,128]{2,1,0:T(8,128)(2,1)S(1)}, u32[]{:S(2)}, u32[]{:S(2)}) %collective-permute-start) | collective-permute-done | bytes 1048608 | tf_op jit(solution)/shard_map/ppermute | solution.py:127
  336.1 24.9 %collective-permute-done.1 = bf16[64,64,128]{2,1,0:T(8,128)(2,1)S(1)} collective-permute-done((bf16[64,64,128]{2,1,0:T(8,128)(2,1)S(1)}, bf16[64,64,128]{2,1,0:T(8,128)(2,1)S(1)}, u32[]{:S(2)}, u32[]{:S(2)}) %collective-permute-start.1) | collective-permute-done | bytes 1048608 | tf_op jit(solution)/shard_map/ppermute | solution.py:127
  361.0 3.5 fusion
Async XLA Ops:
  0.9 2.2 copy-start
  3.1 1.6 copy-start.1
  15.1 218.2 %copy-start.2 = (s32[4]{0:T(128)S(1)}, s32[4]{0:T(128)}, u32[]{:S(2)}) copy-start(s32[4]{0:T(128)} %shift_ref.1) | copy-start | bytes 52
  15.1 218.2 %copy-start.3 = (f32[4]{0:T(128)S(1)}, f32[4]{0:T(128)}, u32[]{:S(2)}) copy-start(f32[4]{0:T(128)} %occupation_ref.1) | copy-start | bytes 52
  233.3 19.4 %copy-start.4 = (f32[1,3]{1,0:T(1,128)S(1)}, f32[1,3]{1,0:T(1,128)}, u32[]{:S(2)}) copy-start(f32[1,3]{1,0:T(1,128)} %param.11) | copy-start | bytes 40
  237.6 98.5 %collective-permute-start = (bf16[64,64,128]{2,1,0:T(8,128)(2,1)S(1)}, bf16[64,64,128]{2,1,0:T(8,128)(2,1)S(1)}, u32[]{:S(2)}, u32[]{:S(2)}) collective-permute-start(bf16[64,64,128]{2,1,0:T(8,128)(2,1)S(1)} %energy_mix.1), channel_id=1, source_target_pairs={{0,1},{1,2},{2,3},{3,4},{4,5},{5,6},{6,7},{7,8},{8,9},{9,10},{10,1... | collective-permute-start | bytes 3145736 | tf_op jit(solution)/shard_map/ppermute | solution.py:127
  250.8 110.3 %collective-permute-start.1 = (bf16[64,64,128]{2,1,0:T(8,128)(2,1)S(1)}, bf16[64,64,128]{2,1,0:T(8,128)(2,1)S(1)}, u32[]{:S(2)}, u32[]{:S(2)}) collective-permute-start(bf16[64,64,128]{2,1,0:T(8,128)(2,1)S(1)} %energy_mix.1), channel_id=1, source_target_pairs={{0,15},{1,0},{2,1},{3,2},{4,3},{5,4},{6,5},{7,6},{8,7},{9,8},{10,9... | collective-permute-start | bytes 3145736 | tf_op jit(solution)/shard_map/ppermute | solution.py:127

commit v2 on v1

v2 whole, which is shorter than its diff:
```python
import functools

import jax
import jax.numpy as jnp
from jax import lax
from jax.experimental import pallas as pl
from jax.experimental.pallas import tpu as pltpu
from jax.sharding import PartitionSpec as P


ATOMS_PER_STEP = 8
ENERGIES_PER_STEP = 4
HEAD = 32


def sandwich_kernel(slots, neighbours_ref, green_ref, bond_ref, out_ref, stacked):
    per_step, orbitals = bond_ref.shape[0], bond_ref.shape[-1]
    group = pl.program_id(0)
    for local in range(per_step):
        atom = group * per_step + local
        lefts = []
        for slot in range(slots):
            source = neighbours_ref[slot, atom]
            blocks = jnp.concatenate([green_ref[0, source], green_ref[1, source]], axis=1)
            lefts.append(
                jnp.dot(
                    bond_ref[local, slot], blocks, preferred_element_type=jnp.float32
                ).astype(jnp.bfloat16)
            )
        buffer = stacked.at[local % 2]
        for part in range(4):
            columns = slice(part * orbitals, (part + 1) * orbitals)
            for pair in range(slots // 2):
                buffer[columns, 2 * pair * orbitals : 2 * (pair + 1) * orbitals] = jnp.concatenate(
                    [lefts[2 * pair][:, columns], lefts[2 * pair + 1][:, columns]], axis=1
                )
        gradient = jnp.concatenate([bond_ref[local, slot] for slot in range(slots)], axis=1)
        total = lax.dot_general(
            buffer[...],
            gradient,
            (((1,), (1,)), ((), ())),
            preferred_element_type=jnp.float32,
        ).astype(jnp.bfloat16)
        for kind in range(2):
            start = 2 * kind * orbitals
            out_ref[local, kind] = jnp.concatenate(
                [total[start : start + orbitals], total[start + orbitals : start + 2 * orbitals]],
                axis=1,
            )


def sandwich(green, bond_grad, neighbours):
    kinds, atoms, orbitals, width = green.shape
    slots = bond_grad.shape[1]
    per_step = ATOMS_PER_STEP
    block = pl.BlockSpec((per_step, kinds, orbitals, width), lambda i, n: (i, 0, 0, 0))
    return pl.pallas_call(
        functools.partial(sandwich_kernel, slots),
        grid_spec=pltpu.PrefetchScalarGridSpec(
            num_scalar_prefetch=1,
            grid=(atoms // per_step,),
            in_specs=[
                pl.BlockSpec(
                    (kinds, atoms, orbitals, width),
                    lambda i, n: (0, 0, 0, 0),
                    pipeline_mode=pl.Buffered(1),
                ),
                pl.BlockSpec((per_step, slots, orbitals, orbitals), lambda i, n: (i, 0, 0, 0)),
            ],
            out_specs=block,
            scratch_shapes=[pltpu.VMEM((2, 4 * orbitals, slots * orbitals), jnp.bfloat16)],
        ),
        out_shape=jax.ShapeDtypeStruct((atoms, kinds, orbitals, width), jnp.bfloat16),
        compiler_params=pltpu.CompilerParams(vmem_limit_bytes=60 << 20),
        name="sandwich",
    )(neighbours.T, green, bond_grad)


def energy_kernel(modes, first, per_step, energies, shift_ref, occupation_ref, moved_ref, out_ref):
    _, _, rows, width = moved_ref.shape
    start = first + pl.program_id(0) * per_step
    for local in range(per_step):
        energy = start + local
        total = jnp.zeros((rows, width), jnp.float32)
        for mode in range(modes):
            shift = shift_ref[mode]
            filled = occupation_ref[mode]
            below, above = energy - shift, energy + shift
            down_on = jnp.where(below >= 0, 1.0, 0.0)
            up_on = jnp.where(above < energies, 1.0, 0.0)
            down = moved_ref[jnp.maximum(below, 0)].astype(jnp.float32)
            up = moved_ref[jnp.minimum(above, energies - 1)].astype(jnp.float32)
            total = total + ((filled + 1.0) * down_on) * down[1] - (filled * down_on) * down[0]
            total = total + (filled * up_on) * up[1] - ((filled + 1.0) * up_on) * up[0]
        out_ref[local] = total.astype(jnp.bfloat16)


def energy_mix(moved, occupation, energy_shift, first, count):
    energies, kinds, rows, width = moved.shape
    per_step = ENERGIES_PER_STEP
    return pl.pallas_call(
        functools.partial(energy_kernel, occupation.shape[0], first, per_step, energies),
        grid_spec=pltpu.PrefetchScalarGridSpec(
            num_scalar_prefetch=2,
            grid=(count // per_step,),
            in_specs=[
                pl.BlockSpec((energies, kinds, rows, width), lambda i, s, o: (0, 0, 0, 0))
            ],
            out_specs=pl.BlockSpec((per_step, rows, width), lambda i, s, o: (i, 0, 0)),
        ),
        out_shape=jax.ShapeDtypeStruct((count, rows, width), jnp.bfloat16),
        compiler_params=pltpu.CompilerParams(vmem_limit_bytes=32 << 20),
        cost_estimate=pl.CostEstimate(
            flops=32 * count * rows * width, bytes_accessed=6 << 20, transcendentals=0
        ),
        name="energy_mix",
    )(energy_shift, occupation, moved)


def partial_kernel(weight_ref, own_ref, core_ref, out_ref):
    own_weight, core_weight = weight_ref[0], weight_ref[1]

    @pl.loop(0, own_ref.shape[0])
    def _(energy):
        out_ref[energy] = own_weight * own_ref[energy].astype(jnp.float32) + core_weight * (
            core_ref[energy].astype(jnp.float32)
        )


def partial_mix(weights, own, core):
    vmem = pl.BlockSpec(memory_space=pltpu.VMEM)
    return pl.pallas_call(
        partial_kernel,
        in_specs=[pl.BlockSpec(memory_space=pltpu.SMEM), vmem, vmem],
        out_specs=vmem,
        out_shape=jax.ShapeDtypeStruct(own.shape, jnp.float32),
        compiler_params=pltpu.CompilerParams(vmem_limit_bytes=16 << 20),
        name="partial_mix",
    )(weights, own, core)


def combine_kernel(weight_ref, partial_a, partial_b, far_a, far_b, relayed_b, out_ref):
    far_weight = weight_ref[2]
    head = partial_a.shape[0]

    @pl.loop(0, head)
    def _(energy):
        far = far_a[energy].astype(jnp.float32)
        out_ref[energy] = (partial_a[energy] + far_weight * far).astype(jnp.bfloat16)

    @pl.loop(0, partial_b.shape[0])
    def _(energy):
        far = far_b[energy].astype(jnp.float32) + relayed_b[energy].astype(jnp.float32)
        out_ref[head + energy] = (partial_b[energy] + far_weight * far).astype(jnp.bfloat16)


def combine(weights, partial_a, partial_b, far_a, far_b, relayed_b):
    vmem = pl.BlockSpec(memory_space=pltpu.VMEM)
    (head, rows, width), tail = partial_a.shape, partial_b.shape[0]
    return pl.pallas_call(
        combine_kernel,
        in_specs=[pl.BlockSpec(memory_space=pltpu.SMEM)] + [vmem] * 5,
        out_specs=vmem,
        out_shape=jax.ShapeDtypeStruct((head + tail, rows, width), jnp.bfloat16),
        compiler_params=pltpu.CompilerParams(vmem_limit_bytes=16 << 20),
        name="combine",
    )(weights, partial_a, partial_b, far_a, far_b, relayed_b)


def swaps(pairs):
    return [move for one, other in pairs for move in ((one, other), (other, one))]


def exchange(own_a, own_b):
    count = lax.axis_size("mom")
    half = count // 2
    on_chip = swaps([(k, k + 1) for k in range(0, count, 2)])
    far = [(k, (k + 1) % count) for k in range(1, count, 2)]
    long = [(half - 1, half), (count - 1, 0)]
    near = [pair for pair in far if pair not in long]
    helper = {half - 1: half - 3, half: half + 2, count - 1: count - 3, 0: 2}
    out = list(helper.items())
    across = [(helper[one], other) for one, other in swaps(long)]
    relay = lax.ppermute(own_b, "mom", out)
    far_a = lax.ppermute(own_a, "mom", swaps(far))
    relayed_b = lax.ppermute(relay, "mom", across)
    far_b = lax.ppermute(own_b, "mom", swaps(near))
    core_a = lax.ppermute(own_a, "mom", on_chip)
    core_b = lax.ppermute(own_b, "mom", on_chip)
    return core_a, core_b, far_a, far_b, relayed_b


def on_device(green_blocks, bond_grad, neighbours, occupation, energy_shift, mom_weight):
    local_part = sandwich(green_blocks[:, 0, 0], bond_grad, neighbours)
    moved = lax.all_to_all(local_part, "energy", split_axis=0, concat_axis=0, tiled=True)
    own_b = energy_mix(moved, occupation, energy_shift, HEAD, moved.shape[0] - HEAD)
    own_a = energy_mix(moved, occupation, energy_shift, 0, HEAD)
    even = lax.axis_index("mom") % 2 == 0
    core_weight = jnp.where(even, mom_weight[0, 2], mom_weight[0, 0])
    far_weight = jnp.where(even, mom_weight[0, 0], mom_weight[0, 2])
    weights = jnp.stack([mom_weight[0, 1], core_weight, far_weight])
    core_a, core_b, far_a, far_b, relayed_b = exchange(own_a, own_b)
    partial_a = partial_mix(weights, own_a, core_a)
    partial_b = partial_mix(weights, own_b, core_b)
    return combine(weights, partial_a, partial_b, far_a, far_b, relayed_b)[:, None, None]


def solution(mesh):
    in_specs = (P(None, "energy", "mom", None, None, None), P(), P(), P(), P(), P("mom", None))
    out_specs = P(None, "mom", "energy", None, None)

    return jax.shard_map(
        on_device, mesh=mesh, in_specs=in_specs, out_specs=out_specs, check_vma=False
    )
```

time: 365 us -> 327 us (0.90)
  waiting for transfers between devices: 108 us -> 58.4 us
  starting transfers between devices: 15.1 us -> 23.6 us
  Pallas kernels: 14.8 us -> 22.3 us
  local copies, waits for them, and re-layouts: 5.32 us -> 0.62 us
    ppermute x2 -> x6, waiting for transfers between devices: 108 us -> 58.4 us  [the longest x1 42.9 us: exchange(): far_a = lax.ppermute(own_a, 'mom', swaps(far))]
    ppermute x2 -> x6, starting transfers between devices: 15.1 us -> 23.6 us  [the longest x1 14.1 us: exchange(): far_a = lax.ppermute(own_a, 'mom', swaps(far))]
    pallas_call x1 -> x5, Pallas kernels: 4.31 us -> 9.18 us  [the longest x2 4.83 us: energy_mix(): pl.pallas_call(functools.partial(energy_kernel, occupation.shape[0], firs...]
    unnamed x11 -> x6, local copies, waits for them, and re-layouts: 4.56 us -> 0.01 us
  transfers between devices with their start and end apart: 2 -> 6, of which waited for: 2 -> 2; matrix products, arithmetic and copies ran while one was open for 0% -> 0% of each run, Pallas kernels for 0% -> 1%
where the time goes in v2:
time: 327 us
  blocking collectives  218 us (67%)
  waiting for transfers between devices  58.4 us (18%)
  starting transfers between devices  23.6 us (7%)
  Pallas kernels  22.3 us (7%)
    all_to_all x1, blocking collectives, on_device(): lax.all_to_all(local_part, 'energy', split_axis=0, concat_axis=0, tiled=T...  218 us
    ppermute x1, waiting for transfers between devices, exchange(): far_a = lax.ppermute(own_a, 'mom', swaps(far))  42.9 us
    ppermute x1, waiting for transfers between devices, exchange(): relayed_b = lax.ppermute(relay, 'mom', across)  15.4 us
    ppermute x1, starting transfers between devices, exchange(): far_a = lax.ppermute(own_a, 'mom', swaps(far))  14.1 us
    pallas_call x1, Pallas kernels, sandwich(): pl.pallas_call(functools.partial(sandwich_kernel, slots), grid_spec=pltpu...  13.1 us
  transfers between devices with their start and end apart: 6, of which 2 were waited for; matrix products, arithmetic and copies ran while one was open for 0% of the time, Pallas kernels for 1%

profile of v2, /device:TPU:23, one launch (start us, length us, event | category | flops | bytes accessed | tf_op | source)
XLA Modules:
  0.0 326.6 jit_solution(2828701566375089376)
XLA Ops:
  0.0 13.1 %sandwich.1 = bf16[64,2,64,128]{3,2,1,0:T(8,128)(2,1)} custom-call(s32[4,64]{1,0:T(4,128)} %bitcast.11, bf16[2,64,64,128]{3,2,1,0:T(8,128)(2,1)} %bitcast.10, bf16[64,4,64,64]{3,2,1,0:T(8,128)(2,1)} %bond_ref.1), custom_call_target="tpu_custom_call" | custom-call | tf_op jit(solution)/shard_map/sandwich/pallas_call | solution.py:57
  13.1 0.0 copy-start
  13.1 0.0 copy-start.1
  13.1 218.4 %all_to_all.5.moved_ref = bf16[64,2,64,128]{3,2,1,0:T(8,128)(2,1)S(1)} all-to-all(bf16[64,2,64,128]{3,2,1,0:T(8,128)(2,1)} %sandwich.1), channel_id=1, replica_groups=mesh['energy'=64,'mom'=16] {'energy'}, dimensions={0} | all-to-all | bytes 4194304 | tf_op jit(solution)/shard_map/all_to_all | solution.py:195
  231.5 0.0 copy-done
  231.5 0.0 copy-done.1
  231.5 0.0 copy-start.2
  231.5 2.4 energy_mix.3.own_ref
  233.9 3.3 collective-permute-start.4
  237.1 2.4 energy_mix.2.own_ref
  239.6 1.9 collective-permute-start
  241.5 2.4 collective-permute-start.1
  243.9 14.1 %collective-permute-start.2 = (bf16[32,64,128]{2,1,0:T(8,128)(2,1)S(1)}, bf16[32,64,128]{2,1,0:T(8,128)(2,1)S(1)}, u32[]{:S(2)}, u32[]{:S(2)}) collective-permute-start(bf16[32,64,128]{2,1,0:T(8,128)(2,1)S(1)} %energy_mix.2.own_ref), channel_id=1, source_target_pairs={{1,2},{2,1},{3,4},{4,3},{5,6},{6,5},{7,8},{8,7},{9,10},{10,9},{11,... | collective-permute-start | bytes 1572872 | tf_op jit(solution)/shard_map/ppermute | solution.py:185
  258.0 0.7 collective-permute-start.3
  258.7 0.0 collective-permute-done.4
  258.7 1.3 collective-permute-start.5
  260.0 0.0 copy-done.2
  260.0 0.6 fusion
  263.1 0.7 pad_maximum_fusion.weight_ref
  263.9 0.0 collective-permute-done.core_ref
  263.9 1.4 partial_mix.2.partial_a
  265.2 0.0 collective-permute-done.1.core_ref
  265.2 0.8 partial_mix.3.partial_b
  266.1 42.9 %collective-permute-done.2.far_a = bf16[32,64,128]{2,1,0:T(8,128)(2,1)S(1)} collective-permute-done((bf16[32,64,128]{2,1,0:T(8,128)(2,1)S(1)}, bf16[32,64,128]{2,1,0:T(8,128)(2,1)S(1)}, u32[]{:S(2)}, u32[]{:S(2)}) %collective-permute-start.2) | collective-permute-done | bytes 524320 | tf_op jit(solution)/shard_map/ppermute | solution.py:185
  309.0 0.0 collective-permute-done.3.far_b
  309.0 15.4 %collective-permute-done.5.relayed_b = bf16[32,64,128]{2,1,0:T(8,128)(2,1)S(1)} collective-permute-done((bf16[32,64,128]{2,1,0:T(8,128)(2,1)}, bf16[32,64,128]{2,1,0:T(8,128)(2,1)S(1)}, u32[]{:S(2)}, u32[]{:S(2)}) %collective-permute-start.5) | collective-permute-done | bytes 524320 | tf_op jit(solution)/shard_map/ppermute | solution.py:186
  324.5 2.2 combine.1
Async XLA Ops:
  13.1 218.4 %copy-start = (s32[4]{0:T(128)S(1)}, s32[4]{0:T(128)}, u32[]{:S(2)}) copy-start(s32[4]{0:T(128)} %shift_ref.3) | copy-start | bytes 52
  13.1 218.4 %copy-start.1 = (f32[4]{0:T(128)S(1)}, f32[4]{0:T(128)}, u32[]{:S(2)}) copy-start(f32[4]{0:T(128)} %occupation_ref.3) | copy-start | bytes 52
  231.5 28.6 %copy-start.2 = (f32[1,3]{1,0:T(1,128)S(1)}, f32[1,3]{1,0:T(1,128)}, u32[]{:S(2)}) copy-start(f32[1,3]{1,0:T(1,128)} %param.11) | copy-start | bytes 40
  233.9 24.8 %collective-permute-start.4 = (bf16[32,64,128]{2,1,0:T(8,128)(2,1)S(1)}, bf16[32,64,128]{2,1,0:T(8,128)(2,1)}, u32[]{:S(2)}, u32[]{:S(2)}) collective-permute-start(bf16[32,64,128]{2,1,0:T(8,128)(2,1)S(1)} %energy_mix.3.own_ref), channel_id=1, source_target_pairs={{7,5},{8,10},{15,13},{0,2},{23,21},{24,26},{31,29},{16,18},{39,37}... | collective-permute-start | bytes 1572872 | tf_op jit(solution)/shard_map/ppermute | solution.py:184
  239.6 24.3 %collective-permute-start = (bf16[32,64,128]{2,1,0:T(8,128)(2,1)S(1)}, bf16[32,64,128]{2,1,0:T(8,128)(2,1)}, u32[]{:S(2)}, u32[]{:S(2)}) collective-permute-start(bf16[32,64,128]{2,1,0:T(8,128)(2,1)S(1)} %energy_mix.2.own_ref), channel_id=1, source_target_pairs={{0,1},{1,0},{2,3},{3,2},{4,5},{5,4},{6,7},{7,6},{8,9},{9,8},{10,11... | collective-permute-start | bytes 1572872 | tf_op jit(solution)/shard_map/ppermute | solution.py:188
  241.5 23.7 %collective-permute-start.1 = (bf16[32,64,128]{2,1,0:T(8,128)(2,1)S(1)}, bf16[32,64,128]{2,1,0:T(8,128)(2,1)S(1)}, u32[]{:S(2)}, u32[]{:S(2)}) collective-permute-start(bf16[32,64,128]{2,1,0:T(8,128)(2,1)S(1)} %energy_mix.3.own_ref), channel_id=1, source_target_pairs={{0,1},{1,0},{2,3},{3,2},{4,5},{5,4},{6,7},{7,6},{8,9},{9,8},{10,11... | collective-permute-start | bytes 1572872 | tf_op jit(solution)/shard_map/ppermute | solution.py:189
  243.9 65.1 %collective-permute-start.2 = (bf16[32,64,128]{2,1,0:T(8,128)(2,1)S(1)}, bf16[32,64,128]{2,1,0:T(8,128)(2,1)S(1)}, u32[]{:S(2)}, u32[]{:S(2)}) collective-permute-start(bf16[32,64,128]{2,1,0:T(8,128)(2,1)S(1)} %energy_mix.2.own_ref), channel_id=1, source_target_pairs={{1,2},{2,1},{3,4},{4,3},{5,6},{6,5},{7,8},{8,7},{9,10},{10,9},{11,... | collective-permute-start | bytes 1572872 | tf_op jit(solution)/shard_map/ppermute | solution.py:185
  258.0 51.0 %collective-permute-start.3 = (bf16[32,64,128]{2,1,0:T(8,128)(2,1)S(1)}, bf16[32,64,128]{2,1,0:T(8,128)(2,1)S(1)}, u32[]{:S(2)}, u32[]{:S(2)}) collective-permute-start(bf16[32,64,128]{2,1,0:T(8,128)(2,1)S(1)} %energy_mix.3.own_ref), channel_id=1, source_target_pairs={{1,2},{2,1},{3,4},{4,3},{5,6},{6,5},{9,10},{10,9},{11,12},{12,11},... | collective-permute-start | bytes 1572872 | tf_op jit(solution)/shard_map/ppermute | solution.py:187
  258.7 65.7 %collective-permute-start.5 = (bf16[32,64,128]{2,1,0:T(8,128)(2,1)}, bf16[32,64,128]{2,1,0:T(8,128)(2,1)S(1)}, u32[]{:S(2)}, u32[]{:S(2)}) collective-permute-start(bf16[32,64,128]{2,1,0:T(8,128)(2,1)} %collective-permute-done.4), channel_id=1, source_target_pairs={{5,8},{10,7},{13,0},{2,15},{21,24},{26,23},{29,16},{18,31},{37,40}... | collective-permute-start | bytes 1572872 | tf_op jit(solution)/shard_map/ppermute | solution.py:186

commit v3 on v2

--- a/solution.py
+++ b/solution.py
@@ -8,9 +8,9 @@
 from jax.sharding import PartitionSpec as P
 
 
-ATOMS_PER_STEP = 8
+ATOMS_PER_STEP = 16
 ENERGIES_PER_STEP = 4
-HEAD = 32
+HEAD = 28
 
 
 def sandwich_kernel(slots, neighbours_ref, green_ref, bond_ref, out_ref, stacked):
@@ -27,13 +27,15 @@
                     bond_ref[local, slot], blocks, preferred_element_type=jnp.float32
                 ).astype(jnp.bfloat16)
             )
-        buffer = stacked.at[local % 2]
+        buffer = stacked.at[local]
         for part in range(4):
             columns = slice(part * orbitals, (part + 1) * orbitals)
             for pair in range(slots // 2):
                 buffer[columns, 2 * pair * orbitals : 2 * (pair + 1) * orbitals] = jnp.concatenate(
                     [lefts[2 * pair][:, columns], lefts[2 * pair + 1][:, columns]], axis=1
                 )
+    for local in range(per_step):
+        buffer = stacked.at[local]
         gradient = jnp.concatenate([bond_ref[local, slot] for slot in range(slots)], axis=1)
         total = lax.dot_general(
             buffer[...],
@@ -68,7 +70,7 @@
                 pl.BlockSpec((per_step, slots, orbitals, orbitals), lambda i, n: (i, 0, 0, 0)),
             ],
             out_specs=block,
-            scratch_shapes=[pltpu.VMEM((2, 4 * orbitals, slots * orbitals), jnp.bfloat16)],
+            scratch_shapes=[pltpu.VMEM((per_step, 4 * orbitals, slots * orbitals), jnp.bfloat16)],
         ),
         out_shape=jax.ShapeDtypeStruct((atoms, kinds, orbitals, width), jnp.bfloat16),
         compiler_params=pltpu.CompilerParams(vmem_limit_bytes=60 << 20),

time: 327 us -> 313 us (0.957)
  the two profiles are of different devices: /device:TPU:23 before, /device:TPU:16 now
where the time goes in v3:
time: 313 us
  blocking collectives  219 us (70%)
  waiting for transfers between devices  51.8 us (17%)
  starting transfers between devices  19.7 us (6%)
  Pallas kernels  18 us (6%)
    all_to_all x1, blocking collectives, on_device(): lax.all_to_all(local_part, 'energy', split_axis=0, concat_axis=0, tiled=T...  219 us
    ppermute x1, waiting for transfers between devices, exchange(): far_a = lax.ppermute(own_a, 'mom', swaps(far))  32.6 us
    ppermute x1, waiting for transfers between devices, exchange(): relayed_b = lax.ppermute(relay, 'mom', across)  13.4 us
    ppermute x1, starting transfers between devices, exchange(): far_a = lax.ppermute(own_a, 'mom', swaps(far))  9.64 us
    pallas_call x1, Pallas kernels, sandwich(): pl.pallas_call(functools.partial(sandwich_kernel, slots), grid_spec=pltpu...  8.84 us
  transfers between devices with their start and end apart: 6, of which 3 were waited for; matrix products, arithmetic and copies ran while one was open for 0% of the time, Pallas kernels for 1%

profile of v3, /device:TPU:16, one launch (start us, length us, event | category | flops | bytes accessed | tf_op | source)
XLA Modules:
  0.0 312.8 jit_solution(17504912093911539798)
XLA Ops:
  0.0 8.8 %sandwich.1 = bf16[64,2,64,128]{3,2,1,0:T(8,128)(2,1)} custom-call(s32[4,64]{1,0:T(4,128)} %bitcast.11, bf16[2,64,64,128]{3,2,1,0:T(8,128)(2,1)} %bitcast.10, bf16[64,4,64,64]{3,2,1,0:T(8,128)(2,1)} %bond_ref.1), custom_call_target="tpu_custom_call" | custom-call | tf_op jit(solution)/shard_map/sandwich/pallas_call | solution.py:59
  8.8 0.0 copy-start
  8.8 0.0 copy-start.1
  8.8 219.4 %all_to_all.5.moved_ref = bf16[64,2,64,128]{3,2,1,0:T(8,128)(2,1)S(1)} all-to-all(bf16[64,2,64,128]{3,2,1,0:T(8,128)(2,1)} %sandwich.1), channel_id=1, replica_groups=mesh['energy'=64,'mom'=16] {'energy'}, dimensions={0} | all-to-all | bytes 4194304 | tf_op jit(solution)/shard_map/all_to_all | solution.py:197
  228.3 0.0 copy-done
  228.3 0.0 copy-done.1
  228.3 0.0 copy-start.2
  228.3 2.6 energy_mix.3.own_ref
  230.9 4.2 %collective-permute-start.4 = (bf16[36,64,128]{2,1,0:T(8,128)(2,1)S(1)}, bf16[36,64,128]{2,1,0:T(8,128)(2,1)}, u32[]{:S(2)}, u32[]{:S(2)}) collective-permute-start(bf16[36,64,128]{2,1,0:T(8,128)(2,1)S(1)} %energy_mix.3.own_ref), channel_id=1, source_target_pairs={{7,5},{8,10},{15,13},{0,2},{23,21},{24,26},{31,29},{16,18},{39,37}... | collective-permute-start | bytes 1769480 | tf_op jit(solution)/shard_map/ppermute | solution.py:186
  235.1 1.9 collective-permute-start.1
  237.1 0.7 collective-permute-start.3
  237.8 5.8 %collective-permute-done.4 = bf16[36,64,128]{2,1,0:T(8,128)(2,1)} collective-permute-done((bf16[36,64,128]{2,1,0:T(8,128)(2,1)S(1)}, bf16[36,64,128]{2,1,0:T(8,128)(2,1)}, u32[]{:S(2)}, u32[]{:S(2)}) %collective-permute-start.4) | collective-permute-done | bytes 589856 | tf_op jit(solution)/shard_map/ppermute | solution.py:186
  243.6 1.3 collective-permute-start.5
  244.9 2.2 energy_mix.2.own_ref
  247.1 1.9 collective-permute-start
  249.0 9.6 %collective-permute-start.2 = (bf16[28,64,128]{2,1,0:T(8,128)(2,1)S(1)}, bf16[28,64,128]{2,1,0:T(8,128)(2,1)S(1)}, u32[]{:S(2)}, u32[]{:S(2)}) collective-permute-start(bf16[28,64,128]{2,1,0:T(8,128)(2,1)S(1)} %energy_mix.2.own_ref), channel_id=1, source_target_pairs={{1,2},{2,1},{3,4},{4,3},{5,6},{6,5},{7,8},{8,7},{9,10},{10,9},{11,... | collective-permute-start | bytes 1376264 | tf_op jit(solution)/shard_map/ppermute | solution.py:187
  258.7 0.0 copy-done.2
  258.7 0.6 fusion
  261.8 0.7 pad_maximum_fusion.weight_ref
  262.5 0.0 collective-permute-done.core_ref
  262.5 1.3 partial_mix.2.partial_a
  263.8 0.0 collective-permute-done.1.core_ref
  263.8 0.9 partial_mix.3.partial_b
  264.7 32.6 %collective-permute-done.2.far_a = bf16[28,64,128]{2,1,0:T(8,128)(2,1)S(1)} collective-permute-done((bf16[28,64,128]{2,1,0:T(8,128)(2,1)S(1)}, bf16[28,64,128]{2,1,0:T(8,128)(2,1)S(1)}, u32[]{:S(2)}, u32[]{:S(2)}) %collective-permute-start.2) | collective-permute-done | bytes 458784 | tf_op jit(solution)/shard_map/ppermute | solution.py:187
  297.3 0.0 collective-permute-done.3.far_b
  297.3 13.4 %collective-permute-done.5.relayed_b = bf16[36,64,128]{2,1,0:T(8,128)(2,1)S(1)} collective-permute-done((bf16[36,64,128]{2,1,0:T(8,128)(2,1)}, bf16[36,64,128]{2,1,0:T(8,128)(2,1)S(1)}, u32[]{:S(2)}, u32[]{:S(2)}) %collective-permute-start.5) | collective-permute-done | bytes 589856 | tf_op jit(solution)/shard_map/ppermute | solution.py:188
  310.7 2.2 combine.1
Async XLA Ops:
  8.8 219.5 %copy-start = (s32[4]{0:T(128)S(1)}, s32[4]{0:T(128)}, u32[]{:S(2)}) copy-start(s32[4]{0:T(128)} %shift_ref.3) | copy-start | bytes 52
  8.8 219.5 %copy-start.1 = (f32[4]{0:T(128)S(1)}, f32[4]{0:T(128)}, u32[]{:S(2)}) copy-start(f32[4]{0:T(128)} %occupation_ref.3) | copy-start | bytes 52
  228.3 30.4 %copy-start.2 = (f32[1,3]{1,0:T(1,128)S(1)}, f32[1,3]{1,0:T(1,128)}, u32[]{:S(2)}) copy-start(f32[1,3]{1,0:T(1,128)} %param.11) | copy-start | bytes 40
  230.9 12.6 %collective-permute-start.4 = (bf16[36,64,128]{2,1,0:T(8,128)(2,1)S(1)}, bf16[36,64,128]{2,1,0:T(8,128)(2,1)}, u32[]{:S(2)}, u32[]{:S(2)}) collective-permute-start(bf16[36,64,128]{2,1,0:T(8,128)(2,1)S(1)} %energy_mix.3.own_ref), channel_id=1, source_target_pairs={{7,5},{8,10},{15,13},{0,2},{23,21},{24,26},{31,29},{16,18},{39,37}... | collective-permute-start | bytes 1769480 | tf_op jit(solution)/shard_map/ppermute | solution.py:186
  235.1 28.6 %collective-permute-start.1 = (bf16[36,64,128]{2,1,0:T(8,128)(2,1)S(1)}, bf16[36,64,128]{2,1,0:T(8,128)(2,1)S(1)}, u32[]{:S(2)}, u32[]{:S(2)}) collective-permute-start(bf16[36,64,128]{2,1,0:T(8,128)(2,1)S(1)} %energy_mix.3.own_ref), channel_id=1, source_target_pairs={{0,1},{1,0},{2,3},{3,2},{4,5},{5,4},{6,7},{7,6},{8,9},{9,8},{10,11... | collective-permute-start | bytes 1769480 | tf_op jit(solution)/shard_map/ppermute | solution.py:191
  237.1 60.3 %collective-permute-start.3 = (bf16[36,64,128]{2,1,0:T(8,128)(2,1)S(1)}, bf16[36,64,128]{2,1,0:T(8,128)(2,1)S(1)}, u32[]{:S(2)}, u32[]{:S(2)}) collective-permute-start(bf16[36,64,128]{2,1,0:T(8,128)(2,1)S(1)} %energy_mix.3.own_ref), channel_id=1, source_target_pairs={{1,2},{2,1},{3,4},{4,3},{5,6},{6,5},{9,10},{10,9},{11,12},{12,11},... | collective-permute-start | bytes 1769480 | tf_op jit(solution)/shard_map/ppermute | solution.py:189
  243.6 67.1 %collective-permute-start.5 = (bf16[36,64,128]{2,1,0:T(8,128)(2,1)}, bf16[36,64,128]{2,1,0:T(8,128)(2,1)S(1)}, u32[]{:S(2)}, u32[]{:S(2)}) collective-permute-start(bf16[36,64,128]{2,1,0:T(8,128)(2,1)} %collective-permute-done.4), channel_id=1, source_target_pairs={{5,8},{10,7},{13,0},{2,15},{21,24},{26,23},{29,16},{18,31},{37,40}... | collective-permute-start | bytes 1769480 | tf_op jit(solution)/shard_map/ppermute | solution.py:188
  247.1 15.4 %collective-permute-start = (bf16[28,64,128]{2,1,0:T(8,128)(2,1)S(1)}, bf16[28,64,128]{2,1,0:T(8,128)(2,1)}, u32[]{:S(2)}, u32[]{:S(2)}) collective-permute-start(bf16[28,64,128]{2,1,0:T(8,128)(2,1)S(1)} %energy_mix.2.own_ref), channel_id=1, source_target_pairs={{0,1},{1,0},{2,3},{3,2},{4,5},{5,4},{6,7},{7,6},{8,9},{9,8},{10,11... | collective-permute-start | bytes 1376264 | tf_op jit(solution)/shard_map/ppermute | solution.py:190
  249.0 48.3 %collective-permute-start.2 = (bf16[28,64,128]{2,1,0:T(8,128)(2,1)S(1)}, bf16[28,64,128]{2,1,0:T(8,128)(2,1)S(1)}, u32[]{:S(2)}, u32[]{:S(2)}) collective-permute-start(bf16[28,64,128]{2,1,0:T(8,128)(2,1)S(1)} %energy_mix.2.own_ref), channel_id=1, source_target_pairs={{1,2},{2,1},{3,4},{4,3},{5,6},{6,5},{7,8},{8,7},{9,10},{10,9},{11,... | collective-permute-start | bytes 1376264 | tf_op jit(solution)/shard_map/ppermute | solution.py:187

commit v4 on v3

--- a/solution.py
+++ b/solution.py
@@ -9,8 +9,7 @@
 
 
 ATOMS_PER_STEP = 16
-ENERGIES_PER_STEP = 4
-HEAD = 28
+HEAD = 32
 
 
 def sandwich_kernel(slots, neighbours_ref, green_ref, bond_ref, out_ref, stacked):
@@ -78,11 +77,12 @@
     )(neighbours.T, green, bond_grad)
 
 
-def energy_kernel(modes, first, per_step, energies, shift_ref, occupation_ref, moved_ref, out_ref):
-    _, _, rows, width = moved_ref.shape
-    start = first + pl.program_id(0) * per_step
-    for local in range(per_step):
-        energy = start + local
+def energy_kernel(modes, first, shift_ref, occupation_ref, moved_ref, out_ref):
+    energies, _, rows, width = moved_ref.shape
+
+    @pl.loop(0, out_ref.shape[0])
+    def _(local):
+        energy = first + local
         total = jnp.zeros((rows, width), jnp.float32)
         for mode in range(modes):
             shift = shift_ref[mode]
@@ -98,20 +98,14 @@
 
 
 def energy_mix(moved, occupation, energy_shift, first, count):
-    energies, kinds, rows, width = moved.shape
-    per_step = ENERGIES_PER_STEP
-    return pl.pallas_call(
-        functools.partial(energy_kernel, occupation.shape[0], first, per_step, energies),
-        grid_spec=pltpu.PrefetchScalarGridSpec(
-            num_scalar_prefetch=2,
-            grid=(count // per_step,),
-            in_specs=[
-                pl.BlockSpec((energies, kinds, rows, width), lambda i, s, o: (0, 0, 0, 0))
-            ],
-            out_specs=pl.BlockSpec((per_step, rows, width), lambda i, s, o: (i, 0, 0)),
-        ),
+    _, _, rows, width = moved.shape
+    vmem, smem = pl.BlockSpec(memory_space=pltpu.VMEM), pl.BlockSpec(memory_space=pltpu.SMEM)
+    return pl.pallas_call(
+        functools.partial(energy_kernel, occupation.shape[0], first),
+        in_specs=[smem, smem, vmem],
+        out_specs=vmem,
         out_shape=jax.ShapeDtypeStruct((count, rows, width), jnp.bfloat16),
-        compiler_params=pltpu.CompilerParams(vmem_limit_bytes=32 << 20),
+        compiler_params=pltpu.CompilerParams(vmem_limit_bytes=16 << 20),
         cost_estimate=pl.CostEstimate(
             flops=32 * count * rows * width, bytes_accessed=6 << 20, transcendentals=0
         ),

time: 313 us -> 323 us (1.032)
  the two profiles are of different devices: /device:TPU:16 before, /device:TPU:23 now
where the time goes in v4:
time: 323 us
  blocking collectives  218 us (67%)
  waiting for transfers between devices  58.4 us (18%)
  starting transfers between devices  23.6 us (7%)
  Pallas kernels  18.4 us (6%)
    all_to_all x1, blocking collectives, on_device(): lax.all_to_all(local_part, 'energy', split_axis=0, concat_axis=0, tiled=T...  218 us
    ppermute x1, waiting for transfers between devices, exchange(): far_a = lax.ppermute(own_a, 'mom', swaps(far))  42.9 us
    ppermute x1, waiting for transfers between devices, exchange(): relayed_b = lax.ppermute(relay, 'mom', across)  15.4 us
    ppermute x1, starting transfers between devices, exchange(): far_a = lax.ppermute(own_a, 'mom', swaps(far))  14.1 us
    pallas_call x1, Pallas kernels, sandwich(): pl.pallas_call(functools.partial(sandwich_kernel, slots), grid_spec=pltpu...  8.83 us
  transfers between devices with their start and end apart: 6, of which 2 were waited for; matrix products, arithmetic and copies ran while one was open for 0% of the time, Pallas kernels for 1%

profile of v4, /device:TPU:23, one launch (start us, length us, event | category | flops | bytes accessed | tf_op | source)
XLA Modules:
  0.0 322.7 jit_solution(11014282915908397443)
XLA Ops:
  0.0 8.8 %sandwich.1 = bf16[64,2,64,128]{3,2,1,0:T(8,128)(2,1)} custom-call(s32[4,64]{1,0:T(4,128)} %bitcast.11, bf16[2,64,64,128]{3,2,1,0:T(8,128)(2,1)} %bitcast.10, bf16[64,4,64,64]{3,2,1,0:T(8,128)(2,1)} %bond_ref.1), custom_call_target="tpu_custom_call" | custom-call | tf_op jit(solution)/shard_map/sandwich/pallas_call | solution.py:58
  8.8 0.0 copy-start
  8.8 0.0 copy-start.1
  8.8 218.4 %all_to_all.5.moved_ref = bf16[64,2,64,128]{3,2,1,0:T(8,128)(2,1)S(1)} all-to-all(bf16[64,2,64,128]{3,2,1,0:T(8,128)(2,1)} %sandwich.1), channel_id=1, replica_groups=mesh['energy'=64,'mom'=16] {'energy'}, dimensions={0} | all-to-all | bytes 4194304 | tf_op jit(solution)/shard_map/all_to_all | solution.py:191
  227.2 0.0 copy-done
  227.2 0.0 copy-done.1
  227.2 0.0 copy-start.2
  227.2 2.6 energy_mix.3.own_ref
  229.8 3.3 %collective-permute-start.4 = (bf16[32,64,128]{2,1,0:T(8,128)(2,1)S(1)}, bf16[32,64,128]{2,1,0:T(8,128)(2,1)}, u32[]{:S(2)}, u32[]{:S(2)}) collective-permute-start(bf16[32,64,128]{2,1,0:T(8,128)(2,1)S(1)} %energy_mix.3.own_ref), channel_id=1, source_target_pairs={{7,5},{8,10},{15,13},{0,2},{23,21},{24,26},{31,29},{16,18},{39,37}... | collective-permute-start | bytes 1572872 | tf_op jit(solution)/shard_map/ppermute | solution.py:180
  233.1 2.6 energy_mix.2.own_ref
  235.7 1.9 collective-permute-start
  237.6 2.4 collective-permute-start.1
  240.0 14.1 %collective-permute-start.2 = (bf16[32,64,128]{2,1,0:T(8,128)(2,1)S(1)}, bf16[32,64,128]{2,1,0:T(8,128)(2,1)S(1)}, u32[]{:S(2)}, u32[]{:S(2)}) collective-permute-start(bf16[32,64,128]{2,1,0:T(8,128)(2,1)S(1)} %energy_mix.2.own_ref), channel_id=1, source_target_pairs={{1,2},{2,1},{3,4},{4,3},{5,6},{6,5},{7,8},{8,7},{9,10},{10,9},{11,... | collective-permute-start | bytes 1572872 | tf_op jit(solution)/shard_map/ppermute | solution.py:181
  254.1 0.7 collective-permute-start.3
  254.8 0.0 collective-permute-done.4
  254.8 1.3 collective-permute-start.5
  256.1 0.0 copy-done.2
  256.1 0.6 fusion
  259.2 0.7 pad_maximum_fusion.weight_ref
  260.0 0.0 collective-permute-done.core_ref
  260.0 1.4 partial_mix.2.partial_a
  261.3 0.0 collective-permute-done.1.core_ref
  261.3 0.8 partial_mix.3.partial_b
  262.2 42.9 %collective-permute-done.2.far_a = bf16[32,64,128]{2,1,0:T(8,128)(2,1)S(1)} collective-permute-done((bf16[32,64,128]{2,1,0:T(8,128)(2,1)S(1)}, bf16[32,64,128]{2,1,0:T(8,128)(2,1)S(1)}, u32[]{:S(2)}, u32[]{:S(2)}) %collective-permute-start.2) | collective-permute-done | bytes 524320 | tf_op jit(solution)/shard_map/ppermute | solution.py:181
  305.1 0.0 collective-permute-done.3.far_b
  305.1 15.4 %collective-permute-done.5.relayed_b = bf16[32,64,128]{2,1,0:T(8,128)(2,1)S(1)} collective-permute-done((bf16[32,64,128]{2,1,0:T(8,128)(2,1)}, bf16[32,64,128]{2,1,0:T(8,128)(2,1)S(1)}, u32[]{:S(2)}, u32[]{:S(2)}) %collective-permute-start.5) | collective-permute-done | bytes 524320 | tf_op jit(solution)/shard_map/ppermute | solution.py:182
  320.6 2.2 combine.1
Async XLA Ops:
  8.8 218.4 %copy-start = (s32[4]{0:T(128)S(1)}, s32[4]{0:T(128)}, u32[]{:S(2)}) copy-start(s32[4]{0:T(128)} %shift_ref.3) | copy-start | bytes 52
  8.8 218.4 %copy-start.1 = (f32[4]{0:T(128)S(1)}, f32[4]{0:T(128)}, u32[]{:S(2)}) copy-start(f32[4]{0:T(128)} %occupation_ref.3) | copy-start | bytes 52
  227.2 28.9 %copy-start.2 = (f32[1,3]{1,0:T(1,128)S(1)}, f32[1,3]{1,0:T(1,128)}, u32[]{:S(2)}) copy-start(f32[1,3]{1,0:T(1,128)} %param.11) | copy-start | bytes 40
  229.8 25.0 %collective-permute-start.4 = (bf16[32,64,128]{2,1,0:T(8,128)(2,1)S(1)}, bf16[32,64,128]{2,1,0:T(8,128)(2,1)}, u32[]{:S(2)}, u32[]{:S(2)}) collective-permute-start(bf16[32,64,128]{2,1,0:T(8,128)(2,1)S(1)} %energy_mix.3.own_ref), channel_id=1, source_target_pairs={{7,5},{8,10},{15,13},{0,2},{23,21},{24,26},{31,29},{16,18},{39,37}... | collective-permute-start | bytes 1572872 | tf_op jit(solution)/shard_map/ppermute | solution.py:180
  235.7 24.3 %collective-permute-start = (bf16[32,64,128]{2,1,0:T(8,128)(2,1)S(1)}, bf16[32,64,128]{2,1,0:T(8,128)(2,1)}, u32[]{:S(2)}, u32[]{:S(2)}) collective-permute-start(bf16[32,64,128]{2,1,0:T(8,128)(2,1)S(1)} %energy_mix.2.own_ref), channel_id=1, source_target_pairs={{0,1},{1,0},{2,3},{3,2},{4,5},{5,4},{6,7},{7,6},{8,9},{9,8},{10,11... | collective-permute-start | bytes 1572872 | tf_op jit(solution)/shard_map/ppermute | solution.py:184
  237.6 23.7 %collective-permute-start.1 = (bf16[32,64,128]{2,1,0:T(8,128)(2,1)S(1)}, bf16[32,64,128]{2,1,0:T(8,128)(2,1)S(1)}, u32[]{:S(2)}, u32[]{:S(2)}) collective-permute-start(bf16[32,64,128]{2,1,0:T(8,128)(2,1)S(1)} %energy_mix.3.own_ref), channel_id=1, source_target_pairs={{0,1},{1,0},{2,3},{3,2},{4,5},{5,4},{6,7},{7,6},{8,9},{9,8},{10,11... | collective-permute-start | bytes 1572872 | tf_op jit(solution)/shard_map/ppermute | solution.py:185
  240.0 65.1 %collective-permute-start.2 = (bf16[32,64,128]{2,1,0:T(8,128)(2,1)S(1)}, bf16[32,64,128]{2,1,0:T(8,128)(2,1)S(1)}, u32[]{:S(2)}, u32[]{:S(2)}) collective-permute-start(bf16[32,64,128]{2,1,0:T(8,128)(2,1)S(1)} %energy_mix.2.own_ref), channel_id=1, source_target_pairs={{1,2},{2,1},{3,4},{4,3},{5,6},{6,5},{7,8},{8,7},{9,10},{10,9},{11,... | collective-permute-start | bytes 1572872 | tf_op jit(solution)/shard_map/ppermute | solution.py:181
  254.1 51.0 %collective-permute-start.3 = (bf16[32,64,128]{2,1,0:T(8,128)(2,1)S(1)}, bf16[32,64,128]{2,1,0:T(8,128)(2,1)S(1)}, u32[]{:S(2)}, u32[]{:S(2)}) collective-permute-start(bf16[32,64,128]{2,1,0:T(8,128)(2,1)S(1)} %energy_mix.3.own_ref), channel_id=1, source_target_pairs={{1,2},{2,1},{3,4},{4,3},{5,6},{6,5},{9,10},{10,9},{11,12},{12,11},... | collective-permute-start | bytes 1572872 | tf_op jit(solution)/shard_map/ppermute | solution.py:183
  254.8 65.7 %collective-permute-start.5 = (bf16[32,64,128]{2,1,0:T(8,128)(2,1)}, bf16[32,64,128]{2,1,0:T(8,128)(2,1)S(1)}, u32[]{:S(2)}, u32[]{:S(2)}) collective-permute-start(bf16[32,64,128]{2,1,0:T(8,128)(2,1)} %collective-permute-done.4), channel_id=1, source_target_pairs={{5,8},{10,7},{13,0},{2,15},{21,24},{26,23},{29,16},{18,31},{37,40}... | collective-permute-start | bytes 1572872 | tf_op jit(solution)/shard_map/ppermute | solution.py:182
